TPU v7x, 256 devices: a whole 4x4x8 slice. The times are simulated.
256 devices in a mesh: seq: 8 (over y, core), vocab: 32 (over z, x).
Axes of the slice: x: 4, y: 4, z: 8, core: 2. Of those that a mesh axis runs over, the one named last changes fastest.
Arguments:
- hidden: bfloat16 [2, 1024, 5120], P(None, 'seq'), may hold values from -128 to 128
- head_weight: bfloat16 [5120, 77824], P('seq', 'vocab'), may hold values from -1 to 1
- ref_logits: bfloat16 [2, 1024, 77824], P(None, 'seq', 'vocab'), may hold values from -320 to 320
- token_ids: int32 [2, 1024], P(None, 'seq'), may hold values from 0 to 77823
- end_pos: int32 [2], replicated, may hold values from 512 to 1023
- loss_mask: int32 [2, 1024], P(None, 'seq'), may hold values 0 or 1
- scores: float32 [2], replicated, may hold values from -8 to 8
Outputs:
- logit_grad: bfloat16 [2, 1024, 77824], P(None, 'seq', 'vocab')
- hidden_grad: bfloat16 [2, 1024, 5120], P(None, 'seq', 'vocab')
- advantages: float32 [2, 1024], P(None, 'seq')
All inputs are finite; a program needn't handle non-finite values. No bound on the sum of `loss_mask` on one device may be relied on, other than what follows from the above.
Results may differ from a plain program's by a relative error of at most 0.0039.
The roundings to bfloat16 on the way count: a program that leaves them out, or rounds other values in their place, can miss the bound.
Values may be sent and summed in bfloat16 or wider, within the bound.
No kernel may reach another device: no remote copies, remote signals or barrier semaphores. Data moves between devices by JAX's collectives and lax.ppermute only.
A program may use at most 128 MiB of HBM per device.

v0:
```python
import jax
import jax.numpy as jnp
from jax import lax
from jax.sharding import Mesh, PartitionSpec as P

SEQ = ("y", "c")
VOC = ("z", "x")
BOUNDS = ((0, 256), (256, 512), (512, 640))


def spread(value, axes):
    count = lax.axis_size(axes)
    return lax.all_to_all(jnp.broadcast_to(value[None], (count,) + value.shape), axes, 0, 0)


def per_device(hidden, head_weight, ref_logits, token_ids, end_pos, loss_mask, scores):
    batch, segment, width = hidden.shape
    rows = batch * segment
    depth, vocab_dev = head_weight.shape
    seqs = lax.axis_size(SEQ)
    seq_index = lax.axis_index(SEQ)
    seq_start = seq_index * segment
    vocab_start = lax.axis_index(VOC) * vocab_dev
    heads = [lax.all_gather(head_weight[lo:hi], SEQ, axis=0, tiled=True) for lo, hi in BOUNDS]
    refs = ref_logits.astype(jnp.float32).reshape(rows, vocab_dev)
    ref_top = jnp.max(refs, axis=1)
    ref_lse = ref_top + jnp.log(jnp.sum(jnp.exp(refs - ref_top[:, None]), axis=1))
    states = hidden.reshape(rows, seqs, depth)
    logits = None
    for (lo, hi), head in zip(BOUNDS, heads):
        term = jnp.dot(
            states[:, :, lo:hi].reshape(rows, seqs * (hi - lo)),
            head,
            preferred_element_type=jnp.float32,
        )
        logits = term if logits is None else logits + term
    top = jnp.max(logits, axis=1)
    expo = jnp.exp(logits - top[:, None])
    stats = jnp.stack(
        [top, jnp.sum(expo, axis=1), jnp.sum(expo * (logits - refs), axis=1), ref_lse]
    )
    stats = spread(stats, VOC)
    tops = stats[:, 0]
    top_policy = jnp.max(tops, axis=0)
    scale = jnp.exp(tops - top_policy[None])
    total = jnp.sum(stats[:, 1] * scale, axis=0)
    weighted = jnp.sum(stats[:, 2] * scale, axis=0)
    top_ref = jnp.max(stats[:, 3], axis=0)
    lse_ref = top_ref + jnp.log(jnp.sum(jnp.exp(stats[:, 3] - top_ref[None]), axis=0))
    lse_policy = top_policy + jnp.log(total)
    kl_value = (weighted / total - lse_policy + lse_ref).reshape(batch, segment)
    position = seq_start + lax.broadcasted_iota(jnp.int32, (1, segment), 1)
    live = ((loss_mask == 1) & (position <= end_pos[:, None])).astype(jnp.float32)
    at_end = (position == end_pos[:, None]).astype(jnp.float32)
    reward = -0.01 * kl_value * live + scores[:, None] * at_end
    both = spread(jnp.stack([reward, live]), SEQ)
    rewards, lives = (both[:, 0], both[:, 1])
    upper = (
        lax.broadcasted_iota(jnp.int32, (segment, segment), 0)
        >= lax.broadcasted_iota(jnp.int32, (segment, segment), 1)
    ).astype(jnp.float32)
    suffix = jnp.dot(
        rewards.reshape(seqs * batch, segment), upper, precision=lax.Precision.HIGHEST
    ).reshape(seqs, batch, segment)
    totals = jnp.sum(rewards, axis=2)
    later = (
        lax.broadcasted_iota(jnp.int32, (seqs, seqs, 1), 1)
        > lax.broadcasted_iota(jnp.int32, (seqs, seqs, 1), 0)
    ).astype(jnp.float32)
    carried = jnp.sum(later * totals[None], axis=1)
    returns_all = suffix + carried[:, :, None]
    count = jnp.maximum(jnp.sum(lives), 1.0)
    mean = jnp.sum(lives * returns_all) / count
    var = jnp.sum(lives * returns_all * returns_all) / count - mean * mean
    returns = lax.dynamic_index_in_dim(returns_all, seq_index, 0, keepdims=False)
    advantages = (returns - mean) / jnp.sqrt(var + 1e-05)
    factor = live * advantages / count
    prob = jnp.exp(logits - lse_policy[:, None])
    column = vocab_start + lax.broadcasted_iota(jnp.int32, (1, vocab_dev), 1)
    onehot = (column == token_ids.reshape(rows, 1)).astype(jnp.float32)
    logit_grad = (factor.reshape(rows, 1) * (prob - onehot)).astype(jnp.bfloat16)
    pieces = []
    for (lo, hi), head in zip(BOUNDS[::-1], heads[::-1]):
        part = lax.dot_general(
            head, logit_grad, (((1,), (1,)), ((), ())), preferred_element_type=jnp.float32
        ).reshape(seqs, hi - lo, rows)
        pieces.append(lax.psum_scatter(part, "z", scatter_dimension=0, tiled=False))
    mine = jnp.concatenate(pieces[::-1], axis=0)
    mine = mine.reshape(lax.axis_size("x"), depth // lax.axis_size("x"), rows)
    mine = lax.psum_scatter(mine, "x", scatter_dimension=0, tiled=False)
    hidden_grad = mine.T.reshape(batch, segment, -1).astype(jnp.bfloat16)
    return (logit_grad.reshape(batch, segment, vocab_dev), hidden_grad, advantages)


def solution(mesh):
    chips = mesh.devices.reshape(4, 2, 8, 4)
    fine = Mesh(chips, ("y", "c", "z", "x"))
    in_specs = (
        P(None, SEQ, None),
        P(SEQ, VOC),
        P(None, SEQ, VOC),
        P(None, SEQ),
        P(),
        P(None, SEQ),
        P(),
    )
    out_specs = (P(None, SEQ, VOC), P(None, SEQ, VOC), P(None, SEQ))
    return jax.shard_map(
        per_device, mesh=fine, in_specs=in_specs, out_specs=out_specs, check_vma=False
    )
```

profile of v0, /device:TPU:8, one launch (start us, length us, event | category | flops | bytes accessed | tf_op | source)
XLA Modules:
  0.0 374.6 jit_solution(1781459673582744261)
XLA Ops:
  7.2 0.0 all-gather.4.cloned.1.call-start
  7.2 3.4 fusion.19
  10.6 0.0 all-gather.6.cloned.1.call-start
  10.7 0.7 all-gather.6.cloned.1.call-update
  11.4 0.0 all-gather.8.cloned.1.call-start
  11.4 2.0 slice.42
  13.4 0.5 copy.58
  13.9 0.1 fusion.20
  14.1 1.3 copy.59
  15.4 1.3 copy.60
  16.7 0.2 reduce_max.42
  16.9 0.6 exponential_reduce_fusion
  17.5 54.3 %all-gather.4.cloned.1.call-done = bf16[2048,2432]{1,0:T(8,128)(2,1)} async-done(((bf16[256,2432]{1,0:T(8,128)(2,1)}), bf16[2048,2432]{1,0:T(8,128)(2,1)}) %all-gather.4.cloned.1.call-update) | async-done | bytes 9961488 | tf_op jit(solution)/shard_map/all_gather | solution.py:24
  71.8 8.3 %fusion.22 = f32[256,2432]{1,0:T(8,128)} fusion(bf16[256,2048]{1,0:T(8,128)(2,1)S(1)} %bitcast.124, bf16[2048,2432]{1,0:T(8,128)(2,1)} %all-gather.4.cloned.1.call-done), kind=kOutput, calls=%fused_computation.60 | convolution fusion | flops 2550136832 | bytes 13500416 | tf_op jit(solution)/shard_map/dot_general | solution.py:31
  80.1 53.3 %all-gather.6.cloned.1.call-done = bf16[2048,2432]{1,0:T(8,128)(2,1)} async-done(((bf16[256,2432]{1,0:T(8,128)(2,1)}), bf16[2048,2432]{1,0:T(8,128)(2,1)}) %all-gather.6.cloned.1.call-update) | async-done | bytes 9961488 | tf_op jit(solution)/shard_map/all_gather | solution.py:24
  133.4 8.3 %convolution_add_fusion.1 = f32[256,2432]{1,0:T(8,128)} fusion(f32[256,2432]{1,0:T(8,128)} %fusion.22, bf16[256,2048]{1,0:T(8,128)(2,1)S(1)} %bitcast.123, bf16[2048,2432]{1,0:T(8,128)(2,1)} %all-gather.6.cloned.1.call-done), kind=kOutput, calls=%fused_computation.1 | convolution fusion | flops 2550759424 | bytes 15990784 | tf_op jit(solution)/shard_map/dot_general | solution.py:31
  141.8 31.5 %all-gather.8.cloned.1.call-done = bf16[1024,2432]{1,0:T(8,128)(2,1)} async-done(((bf16[128,2432]{1,0:T(8,128)(2,1)}), bf16[1024,2432]{1,0:T(8,128)(2,1)}) %all-gather.8.cloned.1.call-update) | async-done | bytes 4980752 | tf_op jit(solution)/shard_map/all_gather | solution.py:24
  173.3 4.9 %fusion.21 = (f32[256]{0:T(256)S(1)}, f32[256,2432]{1,0:T(8,128)S(1)}) fusion(f32[256,2432]{1,0:T(8,128)} %convolution_add_fusion.1, bf16[1024,2432]{1,0:T(8,128)(2,1)} %all-gather.8.cloned.1.call-done, bf16[32,8,8,128]{3,2,1,0:T(8,128)(2,1)S(1)} %bitcast.119), kind=kOutput, calls=%fused_computation.59 | convolution fusion | flops 1276313344 | bytes 10486784 | tf_op jit(solution)/shard_map/dot_general | solution.py:31
  178.2 0.9 fusion.2
  179.1 0.7 broadcast_in_dim.4
  179.8 9.8 %all-to-all-start = ((f32[32,4,256]{2,1,0:T(4,128)}), f32[32,4,256]{2,1,0:T(4,128)S(1)}, u32[]{:S(2)}, u32[]{:S(2)}) async-start(f32[32,4,256]{2,1,0:T(4,128)} %broadcast_in_dim.4), calls=%async_computation | async-start | bytes 262144 | tf_op jit(solution)/shard_map/all_to_all | solution.py:13
  189.7 10.8 %all-to-all-done = f32[32,4,256]{2,1,0:T(4,128)S(1)} async-done(((f32[32,4,256]{2,1,0:T(4,128)}), f32[32,4,256]{2,1,0:T(4,128)S(1)}, u32[]{:S(2)}, u32[]{:S(2)}) %all-to-all-start) | async-done | bytes 131104 | tf_op jit(solution)/shard_map/all_to_all | solution.py:13
  200.5 0.1 slice_reduce_fusion.2
  200.7 0.1 fusion.18
  200.8 0.6 broadcast_in_dim.5
  201.4 4.8 %all-to-all-start.1 = ((f32[8,2,2,128]{3,2,1,0:T(2,128)}), f32[8,2,2,128]{3,2,1,0:T(2,128)S(1)}, u32[]{:S(2)}, u32[]{:S(2)}) async-start(f32[8,2,2,128]{3,2,1,0:T(2,128)} %broadcast_in_dim.5), calls=%async_computation.1 | async-start | bytes 32768 | tf_op jit(solution)/shard_map/all_to_all | solution.py:13
  206.2 3.9 %all-to-all-done.1 = f32[8,2,2,128]{3,2,1,0:T(2,128)S(1)} async-done(((f32[8,2,2,128]{3,2,1,0:T(2,128)}), f32[8,2,2,128]{3,2,1,0:T(2,128)S(1)}, u32[]{:S(2)}, u32[]{:S(2)}) %all-to-all-start.1) | async-done | bytes 16416 | tf_op jit(solution)/shard_map/all_to_all | solution.py:13
  210.1 0.6 slice_reduce_fusion
  210.7 0.1 copy.55
  210.8 0.1 multiply_reduce_fusion.1
  211.5 0.8 fusion.15
  213.7 0.8 multiply_convert_fusion
  214.6 1.0 copy-done.3
  215.6 4.0 %convolution_bitcast_fusion.2 = f32[1024,256]{0,1:T(8,128)S(1)} fusion(bf16[256,2432]{1,0:T(8,128)(2,1)S(1)} %multiply_convert_fusion, bf16[1024,2432]{1,0:T(8,128)(2,1)} %all-gather.8.cloned.1.call-done), kind=kOutput, calls=%fused_computation.11 | convolution fusion | flops 1275068416 | bytes 7274496 | tf_op jit(solution)/shard_map/dot_general | solution.py:84
  219.6 1.3 copy.46
  220.9 0.2 reduce-scatter.5.cloned.1.call-start
  221.2 5.5 %convolution_bitcast_fusion.1 = f32[2048,256]{0,1:T(8,128)S(1)} fusion(bf16[256,2432]{1,0:T(8,128)(2,1)S(1)} %copy-done.4, bf16[2048,2432]{1,0:T(8,128)(2,1)} %all-gather.4.cloned.1.call-done), kind=kOutput, calls=%fused_computation.3 | convolution fusion | flops 2550136832 | bytes 13303808 | tf_op jit(solution)/shard_map/dot_general | solution.py:84
  226.7 1.8 copy.44
  228.6 0.0 reduce-scatter.7.cloned.1.call-start
  228.6 5.5 %convolution_bitcast_fusion = f32[2048,256]{0,1:T(8,128)S(1)} fusion(bf16[256,2432]{1,0:T(8,128)(2,1)S(1)} %copy-done.4, bf16[2048,2432]{1,0:T(8,128)(2,1)} %all-gather.6.cloned.1.call-done), kind=kOutput, calls=%fused_computation.2 | convolution fusion | flops 2550136832 | bytes 13303808 | tf_op jit(solution)/shard_map/dot_general | solution.py:84
  234.2 1.9 copy.45
  236.1 0.0 reduce-scatter.11.cloned.1.call-start
  236.1 17.7 %reduce-scatter.9.cloned.1.call-done = f32[1,128,256]{2,1,0:T(8,128)} async-done(((f32[8,128,256]{2,1,0:T(8,128)}), f32[1,128,256]{2,1,0:T(8,128)}) %reduce-scatter.9.cloned.1.call-update) | async-done | bytes 131088 | tf_op jit(solution)/shard_map/reduce_scatter | solution.py:87
  253.8 43.1 %reduce-scatter.5.cloned.1.call-done = f32[1,256,256]{2,1,0:T(8,128)} async-done(((f32[8,256,256]{2,1,0:T(8,128)}), f32[1,256,256]{2,1,0:T(8,128)}) %reduce-scatter.5.cloned.1.call-update) | async-done | bytes 262160 | tf_op jit(solution)/shard_map/reduce_scatter | solution.py:87
  296.9 43.7 %reduce-scatter.7.cloned.1.call-done = f32[1,256,256]{2,1,0:T(8,128)} async-done(((f32[8,256,256]{2,1,0:T(8,128)}), f32[1,256,256]{2,1,0:T(8,128)}) %reduce-scatter.7.cloned.1.call-update) | async-done | bytes 262160 | tf_op jit(solution)/shard_map/reduce_scatter | solution.py:87
  340.6 2.0 pad_maximum_fusion
  342.6 23.7 %reduce-scatter.11.cloned.1.call-done = f32[1,160,256]{2,1,0:T(8,128)} async-done(((f32[4,160,256]{2,1,0:T(8,128)}), f32[1,160,256]{2,1,0:T(8,128)}) %reduce-scatter.11.cloned.1.call-update) | async-done | bytes 163856 | tf_op jit(solution)/shard_map/reduce_scatter | solution.py:90
  366.2 1.6 copy_bitcast_fusion
  (42 shorter events, 0.3 us)
Async XLA Ops:
  7.2 64.6 %all-gather.4.cloned.1.call-start = ((), (), s32[]{:S(2)}) async-start(), calls=%async_computation.6 | async-start | bytes 11206656 | tf_op jit(solution)/shard_map/all_gather | solution.py:24
  10.6 2.8 copy-start.2
  10.6 122.8 %all-gather.6.cloned.1.call-start = ((), (), s32[]{:S(2)}) async-start(), calls=%async_computation.7 | async-start | bytes 11206656 | tf_op jit(solution)/shard_map/all_gather | solution.py:24
  11.4 161.9 %all-gather.8.cloned.1.call-start = ((), (), s32[]{:S(2)}) async-start(), calls=%async_computation.8 | async-start | bytes 5603328 | tf_op jit(solution)/shard_map/all_gather | solution.py:24
  14.1 2.6 copy-start
  16.7 55.2 %copy-start.6 = (bf16[32,8,8,256]{3,1,2,0:T(8,128)(2,1)S(1)}, bf16[32,8,8,256]{3,1,2,0:T(8,128)(2,1)}, u32[]{:S(2)}) copy-start(bf16[32,8,8,256]{3,1,2,0:T(8,128)(2,1)} %copy.59) | copy-start | bytes 3145732
  71.8 61.6 %copy-start.5 = (bf16[32,8,8,256]{3,1,2,0:T(8,128)(2,1)S(1)}, bf16[32,8,8,256]{3,1,2,0:T(8,128)(2,1)}, u32[]{:S(2)}) copy-start(bf16[32,8,8,256]{3,1,2,0:T(8,128)(2,1)} %copy.60) | copy-start | bytes 3145732
  173.3 5.0 %copy-start.1 = (bf16[2,128,2432]{2,1,0:T(8,128)(2,1)S(1)}, bf16[2,128,2432]{2,1,0:T(8,128)(2,1)}, u32[]{:S(2)}) copy-start(bf16[2,128,2432]{2,1,0:T(8,128)(2,1)} %param.9) | copy-start | bytes 3735556
  178.2 22.5 %copy-start.9 = (s32[2,128]{1,0:T(2,128)S(1)}, s32[2,128]{1,0:T(2,128)}, u32[]{:S(2)}) copy-start(s32[2,128]{1,0:T(2,128)} %param.12) | copy-start | bytes 3076
  178.2 22.5 %copy-start.10 = (f32[2]{0:T(128)S(1)}, f32[2]{0:T(128)}, u32[]{:S(2)}) copy-start(f32[2]{0:T(128)} %param.13) | copy-start | bytes 28
  178.2 22.5 %copy-start.11 = (s32[2]{0:T(128)S(1)}, s32[2]{0:T(128)}, u32[]{:S(2)}) copy-start(s32[2]{0:T(128)} %param.11) | copy-start | bytes 28
  178.2 35.5 %copy-start.8 = (s32[2,128]{1,0:T(2,128)S(1)}, s32[2,128]{1,0:T(2,128)}, u32[]{:S(2)}) copy-start(s32[2,128]{1,0:T(2,128)} %param.10) | copy-start | bytes 3076
  179.8 20.7 %all-to-all-start = ((f32[32,4,256]{2,1,0:T(4,128)}), f32[32,4,256]{2,1,0:T(4,128)S(1)}, u32[]{:S(2)}, u32[]{:S(2)}) async-start(f32[32,4,256]{2,1,0:T(4,128)} %broadcast_in_dim.4), calls=%async_computation | async-start | bytes 262144 | tf_op jit(solution)/shard_map/all_to_all | solution.py:13
  201.4 8.7 %all-to-all-start.1 = ((f32[8,2,2,128]{3,2,1,0:T(2,128)}), f32[8,2,2,128]{3,2,1,0:T(2,128)S(1)}, u32[]{:S(2)}, u32[]{:S(2)}) async-start(f32[8,2,2,128]{3,2,1,0:T(2,128)} %broadcast_in_dim.5), calls=%async_computation.1 | async-start | bytes 32768 | tf_op jit(solution)/shard_map/all_to_all | solution.py:13
  206.2 47.6 %reduce-scatter.9.cloned.1.call-start = ((), (), s32[]{:S(2)}) async-start(), calls=%async_computation.11 | async-start | bytes 1179648 | tf_op jit(solution)/shard_map/reduce_scatter | solution.py:87
  213.7 5.9 %copy-start.7 = (f32[1,2,128]{2,0,1:T(1,128)}, f32[1,2,128]{2,0,1:T(1,128)S(1)}, u32[]{:S(2)}) copy-start(f32[1,2,128]{2,0,1:T(1,128)S(1)} %subtract_divide_fusion) | copy-start | bytes 3076
  214.6 1.0 copy-start.3
  219.6 1.6 copy-start.4
  220.9 75.9 %reduce-scatter.5.cloned.1.call-start = ((), (), s32[]{:S(2)}) async-start(), calls=%async_computation.9 | async-start | bytes 2359296 | tf_op jit(solution)/shard_map/reduce_scatter | solution.py:87
  228.6 112.0 %reduce-scatter.7.cloned.1.call-start = ((), (), s32[]{:S(2)}) async-start(), calls=%async_computation.10 | async-start | bytes 2359296 | tf_op jit(solution)/shard_map/reduce_scatter | solution.py:87
  236.1 130.2 %reduce-scatter.11.cloned.1.call-start = ((), (), s32[]{:S(2)}) async-start(), calls=%async_computation.12 | async-start | bytes 819200 | tf_op jit(solution)/shard_map/reduce_scatter | solution.py:90
Sparse Core Ops, SparseCore 0:
  10.7 61.0 all-gather.3
  74.2 59.1 all-gather.5
  135.2 37.9 all-gather.7
  221.0 32.6 reduce-scatter.8
  256.2 40.6 reduce-scatter.4
  299.3 41.2 reduce-scatter.6
  343.1 23.0 reduce-scatter.10
where the time goes:
time: 375 us
  waiting for transfers between devices  283 us (75%)
  matrix products  37.4 us (10%)
  between operations  16.4 us (4%)
  local copies, waits for them, and re-layouts  16 us (4%)
  starting transfers between devices  15 us (4%)
  other arithmetic  7.08 us (2%)
    all_gather x3, waiting for transfers between devices, per_device(): lax.all_gather(head_weight[lo:hi], SEQ, axis=0, tiled=True)  139 us
    reduce_scatter x3, waiting for transfers between devices, per_device(): pieces.append(lax.psum_scatter(part, 'z', scatter_dimension=0, tiled=False))  104 us
    reduce_scatter x1, waiting for transfers between devices, per_device(): mine = lax.psum_scatter(mine, 'x', scatter_dimension=0, tiled=False)  23.7 us
    dot_general x3, matrix products, per_device(): jnp.dot(states[:, :, lo:hi].reshape(rows, seqs * (hi - lo)), head, prefer...  21.5 us
    dot_general x3, matrix products, per_device(): lax.dot_general(head, logit_grad, (((1,), (1,)), ((), ())), preferred_ele...  15 us
    all_to_all x2, waiting for transfers between devices, spread(): lax.all_to_all(jnp.broadcast_to(value[None], (count,) + value.shape), axe...  14.7 us
    all_to_all x2, starting transfers between devices, spread(): lax.all_to_all(jnp.broadcast_to(value[None], (count,) + value.shape), axe...  14.6 us
  transfers between devices with their start and end apart: 9, of which 9 were waited for; matrix products, arithmetic and copies ran while one was open for 10% of the time, Pallas kernels for 0%

commit v1 on v0

--- a/solution.py
+++ b/solution.py
@@ -21,7 +21,12 @@
     seq_index = lax.axis_index(SEQ)
     seq_start = seq_index * segment
     vocab_start = lax.axis_index(VOC) * vocab_dev
-    heads = [lax.all_gather(head_weight[lo:hi], SEQ, axis=0, tiled=True) for lo, hi in BOUNDS]
+    heads = [
+        jnp.concatenate(
+            lax.all_to_all(jnp.stack([head_weight[lo:hi]] * lax.axis_size(SEQ)), SEQ, 0, 0), axis=0
+        )
+        for lo, hi in BOUNDS
+    ]
     refs = ref_logits.astype(jnp.float32).reshape(rows, vocab_dev)
     ref_top = jnp.max(refs, axis=1)
     ref_lse = ref_top + jnp.log(jnp.sum(jnp.exp(refs - ref_top[:, None]), axis=1))

time: 375 us -> 520 us (1.39)
  blocking collectives: 0 us -> 117 us
  starting transfers between devices: 15 us -> 27.6 us
  local copies, waits for them, and re-layouts: 16 us -> 25.6 us
    all_to_all x0 -> x2, waiting for transfers between devices: none -> 144 us  [per_device(): lax.all_to_all(jnp.stack([head_weight[lo:hi]] * lax.axis_size(SEQ)), SEQ,...]
    all_gather x3 -> x0, waiting for transfers between devices: 139 us -> none  [per_device(): lax.all_gather(head_weight[lo:hi], SEQ, axis=0, tiled=True)]
    all_to_all x0 -> x1, blocking collectives: none -> 117 us  [per_device(): lax.all_to_all(jnp.stack([head_weight[lo:hi]] * lax.axis_size(SEQ)), SEQ,...]
    all_to_all x0 -> x2, starting transfers between devices: none -> 13.2 us  [per_device(): lax.all_to_all(jnp.stack([head_weight[lo:hi]] * lax.axis_size(SEQ)), SEQ,...]
    another operation x0 -> x3, local copies, waits for them, and re-layouts: none -> 9.02 us  [per_device(): jnp.stack([head_weight[lo:hi]] * lax.axis_size(SEQ))]
  transfers between devices with their start and end apart: 9 -> 8, of which waited for: 9 -> 8; matrix products, arithmetic and copies ran while one was open for 10% -> 7% of each run, Pallas kernels for 0% -> 0%
where the time goes in v1:
time: 520 us; the launch traced here: 519 us
  waiting for transfers between devices  287 us (55%)
  blocking collectives  117 us (22%)
  matrix products  38 us (7%)
  starting transfers between devices  27.6 us (5%)
  local copies, waits for them, and re-layouts  25.6 us (5%)
  between operations  16 us (3%)
  other arithmetic  8.74 us (2%)
    all_to_all x2, waiting for transfers between devices, per_device(): lax.all_to_all(jnp.stack([head_weight[lo:hi]] * lax.axis_size(SEQ)), SEQ,...  144 us
    all_to_all x1, blocking collectives, per_device(): lax.all_to_all(jnp.stack([head_weight[lo:hi]] * lax.axis_size(SEQ)), SEQ,...  117 us
    reduce_scatter x3, waiting for transfers between devices, per_device(): pieces.append(lax.psum_scatter(part, 'z', scatter_dimension=0, tiled=False))  105 us
    reduce_scatter x1, waiting for transfers between devices, per_device(): mine = lax.psum_scatter(mine, 'x', scatter_dimension=0, tiled=False)  23.7 us
    dot_general x3, matrix products, per_device(): jnp.dot(states[:, :, lo:hi].reshape(rows, seqs * (hi - lo)), head, prefer...  21.8 us
    dot_general x3, matrix products, per_device(): lax.dot_general(head, logit_grad, (((1,), (1,)), ((), ())), preferred_ele...  15.5 us
    all_to_all x2, waiting for transfers between devices, spread(): lax.all_to_all(jnp.broadcast_to(value[None], (count,) + value.shape), axe...  14.4 us
    all_to_all x2, starting transfers between devices, spread(): lax.all_to_all(jnp.broadcast_to(value[None], (count,) + value.shape), axe...  14.3 us
  transfers between devices with their start and end apart: 8, of which 8 were waited for; matrix products, arithmetic and copies ran while one was open for 7% of the time, Pallas kernels for 0%

profile of v1, /device:TPU:8, one launch (start us, length us, event | category | flops | bytes accessed | tf_op | source)
XLA Modules:
  0.0 519.4 jit_solution(12993867322957408198)
XLA Ops:
  7.2 1.1 slice.42
  8.3 2.6 stack.25
  10.9 6.7 %all-to-all-start.2 = ((bf16[8,128,2432]{2,1,0:T(8,128)(2,1)}), bf16[8,128,2432]{2,1,0:T(8,128)(2,1)}, u32[]{:S(2)}, u32[]{:S(2)}) async-start(bf16[8,128,2432]{2,1,0:T(8,128)(2,1)} %stack.25), calls=%async_computation.2 | async-start | bytes 9961472 | tf_op jit(solution)/shard_map/all_to_all | solution.py:26
  17.6 2.9 fusion.22
  20.5 53.9 %all-to-all-done.2 = bf16[8,128,2432]{2,1,0:T(8,128)(2,1)} async-done(((bf16[8,128,2432]{2,1,0:T(8,128)(2,1)}), bf16[8,128,2432]{2,1,0:T(8,128)(2,1)}, u32[]{:S(2)}, u32[]{:S(2)}) %all-to-all-start.2) | async-done | bytes 4980768 | tf_op jit(solution)/shard_map/all_to_all | solution.py:26
  74.4 2.0 stack.24
  76.4 116.5 %all_to_all.25 = bf16[8,256,2432]{2,1,0:T(8,128)(2,1)} all-to-all(bf16[8,256,2432]{2,1,0:T(8,128)(2,1)S(1)} %stack.24), channel_id=1, replica_groups=mesh['y'=4,'c'=2,'z'=8,'x'=4] {'y','c'}, dimensions={0} | all-to-all | bytes 19922944 | tf_op jit(solution)/shard_map/all_to_all | solution.py:26
  192.9 4.4 stack.23
  197.4 6.4 %all-to-all-start = ((bf16[8,256,2432]{2,1,0:T(8,128)(2,1)}), bf16[8,256,2432]{2,1,0:T(8,128)(2,1)}, u32[]{:S(2)}, u32[]{:S(2)}) async-start(bf16[8,256,2432]{2,1,0:T(8,128)(2,1)} %stack.23), calls=%async_computation | async-start | bytes 19922944 | tf_op jit(solution)/shard_map/all_to_all | solution.py:26
  203.8 2.3 copy.73
  206.1 1.5 copy-done.1
  207.7 0.3 reduce_max.42
  208.0 0.6 exponential_reduce_fusion
  208.5 1.7 fusion.23
  210.2 5.4 %convolution_bitcast_fusion = f32[256,2432]{1,0:T(8,128)} fusion(bf16[8,128,2432]{2,1,0:T(8,128)(2,1)} %all-to-all-done.2, bf16[256,8,128]{2,1,0:T(8,128)(2,1)S(1)} %slice.51), kind=kOutput, calls=%fused_computation | convolution fusion | flops 1275068416 | bytes 7995392 | tf_op jit(solution)/shard_map/dot_general | solution.py:36
  215.7 8.1 %convolution_bitcast_fusion.1 = f32[256,2432]{1,0:T(8,128)} fusion(bf16[8,256,2432]{2,1,0:T(8,128)(2,1)} %all_to_all.25, bf16[256,8,256]{2,1,0:T(8,128)(2,1)S(1)} %get-tuple-element.31), kind=kOutput, calls=%fused_computation.1 | convolution fusion | flops 2550136832 | bytes 13500416 | tf_op jit(solution)/shard_map/dot_general | solution.py:36
  223.8 90.2 %all-to-all-done = bf16[8,256,2432]{2,1,0:T(8,128)(2,1)} async-done(((bf16[8,256,2432]{2,1,0:T(8,128)(2,1)}), bf16[8,256,2432]{2,1,0:T(8,128)(2,1)}, u32[]{:S(2)}, u32[]{:S(2)}) %all-to-all-start) | async-done | bytes 9961504 | tf_op jit(solution)/shard_map/all_to_all | solution.py:26
  313.9 8.3 %fusion.24 = (f32[256]{0:T(256)S(1)}, f32[256,2432]{1,0:T(8,128)S(1)}) fusion(f32[256,2432]{1,0:T(8,128)} %convolution_bitcast_fusion, f32[256,2432]{1,0:T(8,128)} %convolution_bitcast_fusion.1, bf16[8,256,2432]{2,1,0:T(8,128)(2,1)} %all-to-all-done, bf16[256,8,256]{2,1,0:T(8,128)(2,1)S(1)} %get-tuple-element.30), kind=kOutput, calls=%fused_computation.63 | convolution fusion | flops 2552004352 | bytes 18482176 | tf_op jit(solution)/shard_map/dot_general | solution.py:36
  322.3 0.9 fusion.4
  323.2 0.5 copy-done.2
  323.7 0.7 broadcast_in_dim.4
  324.4 9.6 %all-to-all-start.3 = ((f32[32,4,256]{2,1,0:T(4,128)}), f32[32,4,256]{2,1,0:T(4,128)S(1)}, u32[]{:S(2)}, u32[]{:S(2)}) async-start(f32[32,4,256]{2,1,0:T(4,128)} %broadcast_in_dim.4), calls=%async_computation.3 | async-start | bytes 262144 | tf_op jit(solution)/shard_map/all_to_all | solution.py:13
  334.0 10.5 %all-to-all-done.3 = f32[32,4,256]{2,1,0:T(4,128)S(1)} async-done(((f32[32,4,256]{2,1,0:T(4,128)}), f32[32,4,256]{2,1,0:T(4,128)S(1)}, u32[]{:S(2)}, u32[]{:S(2)}) %all-to-all-start.3) | async-done | bytes 131104 | tf_op jit(solution)/shard_map/all_to_all | solution.py:13
  344.5 0.1 slice_reduce_fusion.2
  344.7 0.1 fusion.21
  344.8 0.6 broadcast_in_dim.5
  345.4 4.7 all-to-all-start.4
  350.1 3.9 all-to-all-done.4
  354.0 0.6 slice_reduce_fusion
  354.6 0.1 copy.70
  354.7 0.1 multiply_reduce_fusion.1
  355.5 0.8 fusion.18
  357.6 2.5 multiply_convert_fusion
  360.1 4.4 convolution_bitcast_fusion.5
  364.6 1.3 copy.58
  365.9 0.0 reduce-scatter.5.cloned.1.call-start
  365.9 5.5 %convolution_bitcast_fusion.4 = f32[2048,256]{0,1:T(8,128)S(1)} fusion(bf16[256,2432]{1,0:T(8,128)(2,1)S(1)} %multiply_convert_fusion, bf16[2048,2432]{1,0:T(8,128)(2,1)} %bitcast.20), kind=kOutput, calls=%fused_computation.6 | convolution fusion | flops 2550136832 | bytes 13303808 | tf_op jit(solution)/shard_map/dot_general | solution.py:89
  371.5 1.8 copy.56
  373.3 0.0 reduce-scatter.7.cloned.1.call-start
  373.4 5.5 %convolution_bitcast_fusion.3 = f32[2048,256]{0,1:T(8,128)S(1)} fusion(bf16[256,2432]{1,0:T(8,128)(2,1)S(1)} %multiply_convert_fusion, bf16[2048,2432]{1,0:T(8,128)(2,1)} %bitcast.115), kind=kOutput, calls=%fused_computation.5 | convolution fusion | flops 2550136832 | bytes 13303808 | tf_op jit(solution)/shard_map/dot_general | solution.py:89
  379.0 1.9 copy.57
  380.9 0.0 reduce-scatter.11.cloned.1.call-start
  380.9 17.7 %reduce-scatter.9.cloned.1.call-done = f32[1,128,256]{2,1,0:T(8,128)} async-done(((f32[8,128,256]{2,1,0:T(8,128)}), f32[1,128,256]{2,1,0:T(8,128)}) %reduce-scatter.9.cloned.1.call-update) | async-done | bytes 131088 | tf_op jit(solution)/shard_map/reduce_scatter | solution.py:92
  398.6 43.5 %reduce-scatter.5.cloned.1.call-done = f32[1,256,256]{2,1,0:T(8,128)} async-done(((f32[8,256,256]{2,1,0:T(8,128)}), f32[1,256,256]{2,1,0:T(8,128)}) %reduce-scatter.5.cloned.1.call-update) | async-done | bytes 262160 | tf_op jit(solution)/shard_map/reduce_scatter | solution.py:92
  442.1 43.5 %reduce-scatter.7.cloned.1.call-done = f32[1,256,256]{2,1,0:T(8,128)} async-done(((f32[8,256,256]{2,1,0:T(8,128)}), f32[1,256,256]{2,1,0:T(8,128)}) %reduce-scatter.7.cloned.1.call-update) | async-done | bytes 262160 | tf_op jit(solution)/shard_map/reduce_scatter | solution.py:92
  485.6 2.0 pad_maximum_fusion
  487.6 23.7 %reduce-scatter.11.cloned.1.call-done = f32[1,160,256]{2,1,0:T(8,128)} async-done(((f32[4,160,256]{2,1,0:T(8,128)}), f32[1,160,256]{2,1,0:T(8,128)}) %reduce-scatter.11.cloned.1.call-update) | async-done | bytes 163856 | tf_op jit(solution)/shard_map/reduce_scatter | solution.py:95
  511.3 1.6 copy_bitcast_fusion
  (33 shorter events, 0.3 us)
Async XLA Ops:
  10.9 63.5 %all-to-all-start.2 = ((bf16[8,128,2432]{2,1,0:T(8,128)(2,1)}), bf16[8,128,2432]{2,1,0:T(8,128)(2,1)}, u32[]{:S(2)}, u32[]{:S(2)}) async-start(bf16[8,128,2432]{2,1,0:T(8,128)(2,1)} %stack.25), calls=%async_computation.2 | async-start | bytes 9961472 | tf_op jit(solution)/shard_map/all_to_all | solution.py:26
  197.4 116.6 %all-to-all-start = ((bf16[8,256,2432]{2,1,0:T(8,128)(2,1)}), bf16[8,256,2432]{2,1,0:T(8,128)(2,1)}, u32[]{:S(2)}, u32[]{:S(2)}) async-start(bf16[8,256,2432]{2,1,0:T(8,128)(2,1)} %stack.23), calls=%async_computation | async-start | bytes 19922944 | tf_op jit(solution)/shard_map/all_to_all | solution.py:26
  203.8 3.9 copy-start
  206.1 1.5 copy-start.1
  322.2 1.5 copy-start.2
  322.2 22.5 %copy-start.6 = (s32[2,128]{1,0:T(2,128)S(1)}, s32[2,128]{1,0:T(2,128)}, u32[]{:S(2)}) copy-start(s32[2,128]{1,0:T(2,128)} %param.12) | copy-start | bytes 3076
  322.2 22.5 %copy-start.7 = (f32[2]{0:T(128)S(1)}, f32[2]{0:T(128)}, u32[]{:S(2)}) copy-start(f32[2]{0:T(128)} %param.13) | copy-start | bytes 28
  322.2 22.5 %copy-start.8 = (s32[2]{0:T(128)S(1)}, s32[2]{0:T(128)}, u32[]{:S(2)}) copy-start(s32[2]{0:T(128)} %param.11) | copy-start | bytes 28
  322.2 35.4 %copy-start.5 = (s32[2,128]{1,0:T(2,128)S(1)}, s32[2,128]{1,0:T(2,128)}, u32[]{:S(2)}) copy-start(s32[2,128]{1,0:T(2,128)} %param.10) | copy-start | bytes 3076
  324.4 20.1 %all-to-all-start.3 = ((f32[32,4,256]{2,1,0:T(4,128)}), f32[32,4,256]{2,1,0:T(4,128)S(1)}, u32[]{:S(2)}, u32[]{:S(2)}) async-start(f32[32,4,256]{2,1,0:T(4,128)} %broadcast_in_dim.4), calls=%async_computation.3 | async-start | bytes 262144 | tf_op jit(solution)/shard_map/all_to_all | solution.py:13
  345.4 8.6 %all-to-all-start.4 = ((f32[8,2,2,128]{3,2,1,0:T(2,128)}), f32[8,2,2,128]{3,2,1,0:T(2,128)S(1)}, u32[]{:S(2)}, u32[]{:S(2)}) async-start(f32[8,2,2,128]{3,2,1,0:T(2,128)} %broadcast_in_dim.5), calls=%async_computation.4 | async-start | bytes 32768 | tf_op jit(solution)/shard_map/all_to_all | solution.py:13
  350.1 48.5 %reduce-scatter.9.cloned.1.call-start = ((), (), s32[]{:S(2)}) async-start(), calls=%async_computation.11 | async-start | bytes 1179648 | tf_op jit(solution)/shard_map/reduce_scatter | solution.py:92
  357.6 6.9 %copy-start.4 = (f32[1,2,128]{2,0,1:T(1,128)}, f32[1,2,128]{2,0,1:T(1,128)S(1)}, u32[]{:S(2)}) copy-start(f32[1,2,128]{2,0,1:T(1,128)S(1)} %subtract_divide_fusion) | copy-start | bytes 3076
  360.1 13.3 %copy-start.3 = (bf16[256,2432]{1,0:T(8,128)(2,1)}, bf16[256,2432]{1,0:T(8,128)(2,1)S(1)}, u32[]{:S(2)}) copy-start(bf16[256,2432]{1,0:T(8,128)(2,1)S(1)} %multiply_convert_fusion) | copy-start | bytes 3735556
  365.9 76.2 %reduce-scatter.5.cloned.1.call-start = ((), (), s32[]{:S(2)}) async-start(), calls=%async_computation.9 | async-start | bytes 2359296 | tf_op jit(solution)/shard_map/reduce_scatter | solution.py:92
  373.3 112.2 %reduce-scatter.7.cloned.1.call-start = ((), (), s32[]{:S(2)}) async-start(), calls=%async_computation.10 | async-start | bytes 2359296 | tf_op jit(solution)/shard_map/reduce_scatter | solution.py:92
  380.9 130.5 %reduce-scatter.11.cloned.1.call-start = ((), (), s32[]{:S(2)}) async-start(), calls=%async_computation.12 | async-start | bytes 819200 | tf_op jit(solution)/shard_map/reduce_scatter | solution.py:95
Sparse Core Ops, SparseCore 0:
  366.0 32.5 reduce-scatter.8
  401.2 40.8 reduce-scatter.4
  444.7 40.8 reduce-scatter.6
  488.0 23.2 reduce-scatter.10
